TPU v7x, 256 devices: a whole 4x4x8 slice. The times are simulated.
256 devices in a mesh: vert: 16 (over x, z_hi), tm: 16 (over y, z_lo, core).
Axes of the slice: x: 4, y: 4, z: 8 (z_hi: 4, z_lo: 2; z = z_hi * 2 + z_lo), core: 2. Of those that a mesh axis runs over, the one named last changes fastest.
Arguments:
- source: bfloat16 [20480, 2048], P('vert', 'tm'), may hold values from -6 to 6
- band_taps: bfloat16 [2, 2, 65], replicated, may hold values from -0.75 to 0.75
- smooth_taps: bfloat16 [2, 65], replicated, may hold values from 0.0009 to 0.031
- parcel_ids: int32 [3, 20480], P(None, 'vert'), may hold values from 0 to 999, as said below
Outputs:
- envelope_coupling: float32 [16, 2, 1504, 1504], P('tm', None, 'vert')
Inputs may be any that keep to these rules, and one draw needn't show every extreme that they name: `parcel_ids`: row r = 0, 1, 2 gives each vertex's parcel in the atlas of 100, 400 or 1000 parcels (values below that count); every parcel of each atlas has at least one vertex.
All inputs are finite; a program needn't handle non-finite values.
Results may differ from a plain program's by a relative error of at most 0.0053.
Values may be sent and summed in bfloat16 or wider, within the bound.
A program may use at most 64 MiB of HBM per device.

v0:
```python
from functools import partial
import math
import jax
import jax.numpy as jnp
from jax import lax
from jax.sharding import PartitionSpec as P

P1 = 100
P2 = 400
P3 = 1000
BANDS = 2
TAPS = 65
HALF = 32
LAG = 64
LAG_STEP = 1
NLAG = 129
EPSILON = 1e-05


def extended_2(cells, sides, width):
    for axis, dim in sides:
        count = lax.axis_size(axis)
        ends = count - 1
        head = lax.slice_in_dim(cells, 0, width, axis=dim)
        tail = lax.slice_in_dim(cells, cells.shape[dim] - width, cells.shape[dim], axis=dim)
        cells = jnp.concatenate(
            [
                lax.ppermute(tail, axis, [(i, (i + 1) % count) for i in range(ends)]),
                cells,
                lax.ppermute(head, axis, [((i + 1) % count, i) for i in range(ends)]),
            ],
            axis=dim,
        )
    return cells


def toeplitz_band(taps, n_out, n_in):
    period = jnp.concatenate([taps, jnp.zeros((n_in + 1 - taps.shape[0],), taps.dtype)])
    return jnp.tile(period, n_out)[: n_out * n_in].reshape(n_out, n_in)


def resolution_of(parcel):
    first = (parcel >= P1).astype(jnp.int32)
    second = (parcel >= P1 + P2).astype(jnp.int32)
    third = (parcel >= P1 + P2 + P3).astype(jnp.int32)
    return first + second + third


def centered_rows(extended, length):
    level_mean = jnp.mean(extended[:, :, LAG : LAG + length], axis=2, keepdims=True)
    centered = (extended - level_mean).astype(jnp.bfloat16)
    middle = centered[:, :, LAG : LAG + length]
    middle_wide = middle.astype(jnp.float32)
    spread = lax.rsqrt(jnp.mean(middle_wide * middle_wide, axis=2) + EPSILON)
    return (centered, middle, spread)


def make_fold(own_middle, own_spread, owner_start, par_dev, t_dev):
    kernel = own_middle.transpose(1, 0, 2).reshape(BANDS * par_dev, 1, t_dev)
    own_level = resolution_of(owner_start + lax.iota(jnp.int32, par_dev))

    def block_value(visiting, first):
        vis_middle = visiting[:, :, LAG : LAG + t_dev].astype(jnp.float32)
        vis_spread = lax.rsqrt(jnp.mean(vis_middle * vis_middle, axis=2) + EPSILON)
        inner = lax.conv_general_dilated(
            visiting,
            kernel,
            (LAG_STEP,),
            "VALID",
            dimension_numbers=("NCH", "OIH", "NCH"),
            feature_group_count=BANDS,
            preferred_element_type=jnp.float32,
        )
        inner = inner.reshape(par_dev, BANDS, par_dev, NLAG)
        energy = jnp.sum(inner * inner, axis=3).transpose(1, 2, 0)
        scale = own_spread.T[:, :, None] * vis_spread.T[:, None, :] / t_dev
        vis_level = resolution_of(first + lax.iota(jnp.int32, par_dev))
        same = ((own_level[:, None] == vis_level[None, :]) & (own_level[:, None] < 3)).astype(
            jnp.float32
        )
        return energy * scale * scale * same[None] / NLAG

    def guarded(visiting, first):
        result = block_value(visiting, first)
        return result

    def fold_rows(carry, piece, start):
        count = piece.shape[0] // par_dev

        def add_block(block_idx, total):
            first = block_idx * par_dev
            visiting = lax.dynamic_slice_in_dim(piece, block_idx * par_dev, par_dev, 0)
            slot = first // par_dev
            zero = jnp.int32(0)
            return lax.dynamic_update_slice(
                total, guarded(visiting, first)[None], (slot, zero, zero, zero)
            )

        return lax.fori_loop(0, count, add_block, carry)

    return fold_rows


def local(source, band_taps, smooth_taps, parcel_ids):
    vert_dev, t_dev = source.shape
    owners = lax.axis_size("vert")
    total_par = (P1 + P2 + P3 + owners - 1) // owners * owners
    par_dev = total_par // owners
    n_mid = t_dev + 2 * HALF
    n_in = t_dev + 4 * HALF
    first_rows = jax.vmap(partial(toeplitz_band, n_out=n_mid, n_in=n_in))(
        band_taps.reshape(2 * BANDS, TAPS)
    )
    first_mat = first_rows.transpose(2, 0, 1).reshape(n_in, 2 * BANDS * n_mid)
    second_rows = jax.vmap(partial(toeplitz_band, n_out=t_dev, n_in=n_mid))(smooth_taps)
    second_mat = second_rows.transpose(0, 2, 1)
    widened = extended_2(source, (("tm", 1),), 2 * HALF)
    block_rows = math.gcd(vert_dev, 128)

    def filter_block(block):
        wave = jnp.dot(block, first_mat, preferred_element_type=jnp.float32).reshape(
            block_rows, 2, BANDS, n_mid
        )
        power = (wave[:, 0] * wave[:, 0] + wave[:, 1] * wave[:, 1]).astype(jnp.bfloat16)
        return jnp.einsum(
            "vbu,but->vbt", power, second_mat, preferred_element_type=jnp.float32
        ).astype(jnp.bfloat16)

    envelope = lax.map(filter_block, widened.reshape(vert_dev // block_rows, block_rows, n_in))
    flat_env = envelope.reshape(vert_dev, BANDS * t_dev)
    offsets = jnp.array([0, P1, P1 + P2], dtype=jnp.int32)
    global_ids = parcel_ids + offsets[:, None]
    owner_start = lax.axis_index("vert") * par_dev
    empty = jnp.zeros((owners, BANDS, par_dev, par_dev), jnp.float32)

    def one_block(block_idx):
        wanted = block_idx * par_dev + lax.iota(jnp.int32, par_dev)
        hits = jnp.sum(
            (global_ids[:, None, :] == wanted[None, :, None]).astype(jnp.bfloat16), axis=0
        )
        return jnp.dot(hits, flat_env, preferred_element_type=jnp.float32)

    pooled = lax.map(
        one_block, jnp.arange(par_dev * lax.axis_size("vert") // par_dev, dtype=jnp.int32)
    )
    own_sums = lax.psum_scatter(
        pooled.reshape(par_dev * lax.axis_size("vert"), BANDS * t_dev),
        "vert",
        scatter_dimension=0,
        tiled=True,
    )
    own_env = own_sums.reshape(par_dev, BANDS, t_dev)
    own_ext = extended_2(own_env, (("tm", 2),), LAG)
    centered, own_middle, own_spread = centered_rows(own_ext, t_dev)
    fold_rows = make_fold(own_middle, own_spread, owner_start, par_dev, t_dev)
    blocks = fold_rows(empty, lax.all_gather(centered, "vert", axis=0, tiled=True), jnp.int32(0))
    coupling = blocks.transpose(1, 2, 0, 3).reshape(BANDS, par_dev, total_par)
    return coupling[None]


def solution(mesh):
    return jax.shard_map(
        local,
        mesh=mesh,
        in_specs=(P("vert", "tm"), P(), P(), P(None, "vert")),
        out_specs=P("tm", None, "vert", None),
        check_vma=False,
    )
```

profile of v0, /device:TPU:1, one launch (start us, length us, event | category | flops | bytes accessed | tf_op | source)
XLA Modules:
  0.0 328.1 jit_solution(10390628284923040536)
XLA Ops:
  8.5 4.9 %collective-permute-start = (bf16[1280,64]{1,0:T(8,128)(2,1)}, bf16[1280,64]{1,0:T(8,128)(2,1)}, u32[]{:S(2)}, u32[]{:S(2)}) collective-permute-start(bf16[1280,64]{1,0:T(8,128)(2,1)} %get-tuple-element.348), channel_id=1, source_target_pairs={{0,1},{1,2},{2,3},{3,4},{4,5},{5,6},{6,7},{7,8},{8,9},{9,10},{10,1... | collective-permute-start | bytes 491528 | tf_op jit(solution)/shard_map/ppermute | solution.py:28
  24.0 12.1 %while.38 = (s32[]{:T(128)}, bf16[10,128,2,128]{3,2,1,0:T(2,128)(2,1)}, bf16[10,128,256]{2,1,0:T(8,128)(2,1)S(1)}, bf16[256,768]{0,1:T(8,128)(2,1)S(1)}, bf16[2,192,128]{2,1,0:T(8,128)(2,1)S(1)}, /*index=5*/s32[]{:T(128)}) while((s32[]{:T(128)}, bf16[10,128,2,128]{3,2,1,0:T(2,128)(2,1)}, bf16[10,128,256]{2,1,0:T(8,128)(2,1)S(1)}, ...), condition=%wide.region_1.2_spmd, body=%wide.region_0.1_spmd.sunk | while | flops 63143936 | bytes 1540681 | solution.py:129
  37.3 27.9 %while.39 = (s32[]{:T(128)}, f32[16,94,256]{2,1,0:T(8,128)S(1)}, s32[3,1280]{1,0:T(4,128)S(1)}, s32[16]{0:T(128)S(1)}, bf16[1280,256]{1,0:T(8,128)(2,1)S(1)}, /*index=5*/s32[]{:T(128)}, s32[1]{0:T(128)}) while((s32[]{:T(128)}, f32[16,94,256]{2,1,0:T(8,128)S(1)}, s32[3,1280]{1,0:T(4,128)S(1)}, s32[16]{0:T(128)S(1)}, ...), condition=%wide.region_4.5_spmd, body=%wide.region_2.4_spmd.sunk | while | flops 62566496 | bytes 1256285 | solution.py:143
  65.3 55.7 %fusion.2 = f32[96,256]{1,0:T(8,128)S(1)} fusion(f32[1504,256]{1,0:T(8,128)S(1)} %reshape.143), kind=kCustom, calls=%all-reduce-scatter | all-reduce-scatter fusion | flops 393217 | bytes 1639424
  124.7 7.9 %collective-permute-start.2 = (f32[94,2,64]{2,1,0:T(2,128)S(1)}, f32[94,2,64]{2,1,0:T(2,128)S(1)}, u32[]{:S(2)}, u32[]{:S(2)}) collective-permute-start(f32[94,2,64]{2,1,0:T(2,128)S(1)} %get-tuple-element.350), channel_id=1, source_target_pairs={{0,1},{1,2},{2,3},{3,4},{4,5},{5,6},{6,7},{7,8},{8,9},{9,10},{10,1... | collective-permute-start | bytes 144392 | tf_op jit(solution)/shard_map/ppermute | solution.py:28
  135.0 3.6 %collective-permute-done.3 = f32[94,2,64]{2,1,0:T(2,128)S(1)} collective-permute-done((f32[94,2,64]{2,1,0:T(2,128)S(1)}, f32[94,2,64]{2,1,0:T(2,128)S(1)}, u32[]{:S(2)}, u32[]{:S(2)}) %collective-permute-start.3) | collective-permute-done | bytes 48160 | tf_op jit(solution)/shard_map/ppermute | solution.py:30
  142.8 54.5 %all-gather.2.cloned.1.call-done = bf16[1504,2,256]{2,1,0:T(2,128)(2,1)} async-done(((bf16[94,2,256]{2,1,0:T(2,128)(2,1)}), bf16[1504,2,256]{2,1,0:T(2,128)(2,1)}) %all-gather.2.cloned.1.call-update) | async-done | bytes 1540112 | tf_op jit(solution)/shard_map/all_gather | solution.py:156
  198.7 117.5 %while.40 = (s32[]{:T(128)}, f32[16,2,94,94]{3,2,1,0:T(8,128)}, bf16[1504,2,256]{2,1,0:T(2,128)(2,1)}, bf16[188,1,128]{0,2,1:T(8,128)(2,1)S(1)}, f32[94,2]{0,1:T...) while((s32[]{:T(128)}, f32[16,2,94,94]{3,2,1,0:T(8,128)}, ...), condition=%wide.region_11.12_spmd.clone, body=%wide.region_8.11_spmd.clone.sunk | while | flops 1172045696 | bytes 1180199 | solution.py:99
  199.8 4.9 %multiply_reduce_fusion.5 = f32[94,188]{1,0:T(8,128)S(1)} fusion(bf16[94,2,256]{0,1,2:T(2,128)(2,1)S(1)} %copy.64, s32[188]{0:T(256)S(1)} %get-tuple-element.532, bf16[188,128]{0,1:T(8,128)(2,1)S(1)} %bitcast.104), kind=kOutput, calls=%fused_computation.18.clone.1 | convolution fusion | flops 1171838208 | bytes 215824 | tf_op jit(solution)/shard_map/while/body/eval_jaxpr/conv_general_dilated | solution.py:65
  207.1 4.9 %multiply_reduce_fusion.5 = f32[94,188]{1,0:T(8,128)S(1)} fusion(bf16[94,2,256]{0,1,2:T(2,128)(2,1)S(1)} %copy.64, s32[188]{0:T(256)S(1)} %get-tuple-element.532, bf16[188,128]{0,1:T(8,128)(2,1)S(1)} %bitcast.104), kind=kOutput, calls=%fused_computation.18.clone.1 | convolution fusion | flops 1171838208 | bytes 215824 | tf_op jit(solution)/shard_map/while/body/eval_jaxpr/conv_general_dilated | solution.py:65
  214.5 4.9 %multiply_reduce_fusion.5 = f32[94,188]{1,0:T(8,128)S(1)} fusion(bf16[94,2,256]{0,1,2:T(2,128)(2,1)S(1)} %copy.64, s32[188]{0:T(256)S(1)} %get-tuple-element.532, bf16[188,128]{0,1:T(8,128)(2,1)S(1)} %bitcast.104), kind=kOutput, calls=%fused_computation.18.clone.1 | convolution fusion | flops 1171838208 | bytes 215824 | tf_op jit(solution)/shard_map/while/body/eval_jaxpr/conv_general_dilated | solution.py:65
  221.8 4.9 %multiply_reduce_fusion.5 = f32[94,188]{1,0:T(8,128)S(1)} fusion(bf16[94,2,256]{0,1,2:T(2,128)(2,1)S(1)} %copy.64, s32[188]{0:T(256)S(1)} %get-tuple-element.532, bf16[188,128]{0,1:T(8,128)(2,1)S(1)} %bitcast.104), kind=kOutput, calls=%fused_computation.18.clone.1 | convolution fusion | flops 1171838208 | bytes 215824 | tf_op jit(solution)/shard_map/while/body/eval_jaxpr/conv_general_dilated | solution.py:65
  229.2 4.9 %multiply_reduce_fusion.5 = f32[94,188]{1,0:T(8,128)S(1)} fusion(bf16[94,2,256]{0,1,2:T(2,128)(2,1)S(1)} %copy.64, s32[188]{0:T(256)S(1)} %get-tuple-element.532, bf16[188,128]{0,1:T(8,128)(2,1)S(1)} %bitcast.104), kind=kOutput, calls=%fused_computation.18.clone.1 | convolution fusion | flops 1171838208 | bytes 215824 | tf_op jit(solution)/shard_map/while/body/eval_jaxpr/conv_general_dilated | solution.py:65
  236.5 4.9 %multiply_reduce_fusion.5 = f32[94,188]{1,0:T(8,128)S(1)} fusion(bf16[94,2,256]{0,1,2:T(2,128)(2,1)S(1)} %copy.64, s32[188]{0:T(256)S(1)} %get-tuple-element.532, bf16[188,128]{0,1:T(8,128)(2,1)S(1)} %bitcast.104), kind=kOutput, calls=%fused_computation.18.clone.1 | convolution fusion | flops 1171838208 | bytes 215824 | tf_op jit(solution)/shard_map/while/body/eval_jaxpr/conv_general_dilated | solution.py:65
  243.9 4.9 %multiply_reduce_fusion.5 = f32[94,188]{1,0:T(8,128)S(1)} fusion(bf16[94,2,256]{0,1,2:T(2,128)(2,1)S(1)} %copy.64, s32[188]{0:T(256)S(1)} %get-tuple-element.532, bf16[188,128]{0,1:T(8,128)(2,1)S(1)} %bitcast.104), kind=kOutput, calls=%fused_computation.18.clone.1 | convolution fusion | flops 1171838208 | bytes 215824 | tf_op jit(solution)/shard_map/while/body/eval_jaxpr/conv_general_dilated | solution.py:65
  251.2 4.9 %multiply_reduce_fusion.5 = f32[94,188]{1,0:T(8,128)S(1)} fusion(bf16[94,2,256]{0,1,2:T(2,128)(2,1)S(1)} %copy.64, s32[188]{0:T(256)S(1)} %get-tuple-element.532, bf16[188,128]{0,1:T(8,128)(2,1)S(1)} %bitcast.104), kind=kOutput, calls=%fused_computation.18.clone.1 | convolution fusion | flops 1171838208 | bytes 215824 | tf_op jit(solution)/shard_map/while/body/eval_jaxpr/conv_general_dilated | solution.py:65
  258.6 4.9 %multiply_reduce_fusion.5 = f32[94,188]{1,0:T(8,128)S(1)} fusion(bf16[94,2,256]{0,1,2:T(2,128)(2,1)S(1)} %copy.64, s32[188]{0:T(256)S(1)} %get-tuple-element.532, bf16[188,128]{0,1:T(8,128)(2,1)S(1)} %bitcast.104), kind=kOutput, calls=%fused_computation.18.clone.1 | convolution fusion | flops 1171838208 | bytes 215824 | tf_op jit(solution)/shard_map/while/body/eval_jaxpr/conv_general_dilated | solution.py:65
  265.9 4.9 %multiply_reduce_fusion.5 = f32[94,188]{1,0:T(8,128)S(1)} fusion(bf16[94,2,256]{0,1,2:T(2,128)(2,1)S(1)} %copy.64, s32[188]{0:T(256)S(1)} %get-tuple-element.532, bf16[188,128]{0,1:T(8,128)(2,1)S(1)} %bitcast.104), kind=kOutput, calls=%fused_computation.18.clone.1 | convolution fusion | flops 1171838208 | bytes 215824 | tf_op jit(solution)/shard_map/while/body/eval_jaxpr/conv_general_dilated | solution.py:65
  273.3 4.9 %multiply_reduce_fusion.5 = f32[94,188]{1,0:T(8,128)S(1)} fusion(bf16[94,2,256]{0,1,2:T(2,128)(2,1)S(1)} %copy.64, s32[188]{0:T(256)S(1)} %get-tuple-element.532, bf16[188,128]{0,1:T(8,128)(2,1)S(1)} %bitcast.104), kind=kOutput, calls=%fused_computation.18.clone.1 | convolution fusion | flops 1171838208 | bytes 215824 | tf_op jit(solution)/shard_map/while/body/eval_jaxpr/conv_general_dilated | solution.py:65
  280.6 4.9 %multiply_reduce_fusion.5 = f32[94,188]{1,0:T(8,128)S(1)} fusion(bf16[94,2,256]{0,1,2:T(2,128)(2,1)S(1)} %copy.64, s32[188]{0:T(256)S(1)} %get-tuple-element.532, bf16[188,128]{0,1:T(8,128)(2,1)S(1)} %bitcast.104), kind=kOutput, calls=%fused_computation.18.clone.1 | convolution fusion | flops 1171838208 | bytes 215824 | tf_op jit(solution)/shard_map/while/body/eval_jaxpr/conv_general_dilated | solution.py:65
  287.9 4.9 %multiply_reduce_fusion.5 = f32[94,188]{1,0:T(8,128)S(1)} fusion(bf16[94,2,256]{0,1,2:T(2,128)(2,1)S(1)} %copy.64, s32[188]{0:T(256)S(1)} %get-tuple-element.532, bf16[188,128]{0,1:T(8,128)(2,1)S(1)} %bitcast.104), kind=kOutput, calls=%fused_computation.18.clone.1 | convolution fusion | flops 1171838208 | bytes 215824 | tf_op jit(solution)/shard_map/while/body/eval_jaxpr/conv_general_dilated | solution.py:65
  295.3 4.9 %multiply_reduce_fusion.5 = f32[94,188]{1,0:T(8,128)S(1)} fusion(bf16[94,2,256]{0,1,2:T(2,128)(2,1)S(1)} %copy.64, s32[188]{0:T(256)S(1)} %get-tuple-element.532, bf16[188,128]{0,1:T(8,128)(2,1)S(1)} %bitcast.104), kind=kOutput, calls=%fused_computation.18.clone.1 | convolution fusion | flops 1171838208 | bytes 215824 | tf_op jit(solution)/shard_map/while/body/eval_jaxpr/conv_general_dilated | solution.py:65
  302.6 4.9 %multiply_reduce_fusion.5 = f32[94,188]{1,0:T(8,128)S(1)} fusion(bf16[94,2,256]{0,1,2:T(2,128)(2,1)S(1)} %copy.64, s32[188]{0:T(256)S(1)} %get-tuple-element.532, bf16[188,128]{0,1:T(8,128)(2,1)S(1)} %bitcast.104), kind=kOutput, calls=%fused_computation.18.clone.1 | convolution fusion | flops 1171838208 | bytes 215824 | tf_op jit(solution)/shard_map/while/body/eval_jaxpr/conv_general_dilated | solution.py:65
  310.0 4.9 %multiply_reduce_fusion.5 = f32[94,188]{1,0:T(8,128)S(1)} fusion(bf16[94,2,256]{0,1,2:T(2,128)(2,1)S(1)} %copy.64, s32[188]{0:T(256)S(1)} %get-tuple-element.532, bf16[188,128]{0,1:T(8,128)(2,1)S(1)} %bitcast.104), kind=kOutput, calls=%fused_computation.18.clone.1 | convolution fusion | flops 1171838208 | bytes 215824 | tf_op jit(solution)/shard_map/while/body/eval_jaxpr/conv_general_dilated | solution.py:65
  (340 shorter events, 95.9 us)
Async XLA Ops:
  6.5 190.8 %all-gather.2.cloned.1.call-start = ((), (), s32[]{:S(2)}) async-start(), calls=%async_computation | async-start | bytes 1636352 | tf_op jit(solution)/shard_map/all_gather | solution.py:156
  8.5 10.6 %collective-permute-start = (bf16[1280,64]{1,0:T(8,128)(2,1)}, bf16[1280,64]{1,0:T(8,128)(2,1)}, u32[]{:S(2)}, u32[]{:S(2)}) collective-permute-start(bf16[1280,64]{1,0:T(8,128)(2,1)} %get-tuple-element.348), channel_id=1, source_target_pairs={{0,1},{1,2},{2,3},{3,4},{4,5},{5,6},{6,7},{7,8},{8,9},{9,10},{10,1... | collective-permute-start | bytes 491528 | tf_op jit(solution)/shard_map/ppermute | solution.py:28
  13.4 9.1 %collective-permute-start.1 = (bf16[1280,64]{1,0:T(8,128)(2,1)S(1)}, bf16[1280,64]{1,0:T(8,128)(2,1)}, u32[]{:S(2)}, u32[]{:S(2)}) collective-permute-start(bf16[1280,64]{1,0:T(8,128)(2,1)S(1)} %get-tuple-element.349), channel_id=1, source_target_pairs={{1,0},{2,1},{3,2},{4,3},{5,4},{6,5},{7,6},{8,7},{9,8},{10,9},{11,1... | collective-permute-start | bytes 491528 | tf_op jit(solution)/shard_map/ppermute | solution.py:30
  65.3 57.6 %copy-start.3 = (u32[256]{0:T(256)S(1)}, u32[256]{0:T(256)}, u32[]{:S(2)}) copy-start(u32[256]{0:T(256)} %constant.228) | copy-start | bytes 3076
  121.1 3.1 collective-permute-start.4
  124.5 74.1 %copy-start.4 = (s32[188]{0:T(256)S(1)}, s32[188]{0:T(256)}, u32[]{:S(2)}) copy-start(s32[188]{0:T(256)} %constant.197.clone.2) | copy-start | bytes 2260
  124.7 10.2 %collective-permute-start.2 = (f32[94,2,64]{2,1,0:T(2,128)S(1)}, f32[94,2,64]{2,1,0:T(2,128)S(1)}, u32[]{:S(2)}, u32[]{:S(2)}) collective-permute-start(f32[94,2,64]{2,1,0:T(2,128)S(1)} %get-tuple-element.350), channel_id=1, source_target_pairs={{0,1},{1,2},{2,3},{3,4},{4,5},{5,6},{6,7},{7,8},{8,9},{9,10},{10,1... | collective-permute-start | bytes 144392 | tf_op jit(solution)/shard_map/ppermute | solution.py:28
  132.7 5.9 %collective-permute-start.3 = (f32[94,2,64]{2,1,0:T(2,128)S(1)}, f32[94,2,64]{2,1,0:T(2,128)S(1)}, u32[]{:S(2)}, u32[]{:S(2)}) collective-permute-start(f32[94,2,64]{2,1,0:T(2,128)S(1)} %get-tuple-element.351), channel_id=1, source_target_pairs={{1,0},{2,1},{3,2},{4,3},{5,4},{6,5},{7,6},{8,7},{9,8},{10,9},{11,1... | collective-permute-start | bytes 144392 | tf_op jit(solution)/shard_map/ppermute | solution.py:30
  199.8 5.5 %copy-start.1 = (f32[94,2]{0,1:T(2,128)S(1)}, f32[94,2]{0,1:T(2,128)}, u32[]{:S(2)}) copy-start(f32[94,2]{0,1:T(2,128)} %get-tuple-element.524) | copy-start | bytes 2260 | tf_op jit(solution)/shard_map/while
  207.1 5.5 %copy-start.1 = (f32[94,2]{0,1:T(2,128)S(1)}, f32[94,2]{0,1:T(2,128)}, u32[]{:S(2)}) copy-start(f32[94,2]{0,1:T(2,128)} %get-tuple-element.524) | copy-start | bytes 2260 | tf_op jit(solution)/shard_map/while
  214.5 5.5 %copy-start.1 = (f32[94,2]{0,1:T(2,128)S(1)}, f32[94,2]{0,1:T(2,128)}, u32[]{:S(2)}) copy-start(f32[94,2]{0,1:T(2,128)} %get-tuple-element.524) | copy-start | bytes 2260 | tf_op jit(solution)/shard_map/while
  221.8 5.5 %copy-start.1 = (f32[94,2]{0,1:T(2,128)S(1)}, f32[94,2]{0,1:T(2,128)}, u32[]{:S(2)}) copy-start(f32[94,2]{0,1:T(2,128)} %get-tuple-element.524) | copy-start | bytes 2260 | tf_op jit(solution)/shard_map/while
  229.2 5.5 %copy-start.1 = (f32[94,2]{0,1:T(2,128)S(1)}, f32[94,2]{0,1:T(2,128)}, u32[]{:S(2)}) copy-start(f32[94,2]{0,1:T(2,128)} %get-tuple-element.524) | copy-start | bytes 2260 | tf_op jit(solution)/shard_map/while
  236.5 5.5 %copy-start.1 = (f32[94,2]{0,1:T(2,128)S(1)}, f32[94,2]{0,1:T(2,128)}, u32[]{:S(2)}) copy-start(f32[94,2]{0,1:T(2,128)} %get-tuple-element.524) | copy-start | bytes 2260 | tf_op jit(solution)/shard_map/while
  243.9 5.5 %copy-start.1 = (f32[94,2]{0,1:T(2,128)S(1)}, f32[94,2]{0,1:T(2,128)}, u32[]{:S(2)}) copy-start(f32[94,2]{0,1:T(2,128)} %get-tuple-element.524) | copy-start | bytes 2260 | tf_op jit(solution)/shard_map/while
  251.2 5.5 %copy-start.1 = (f32[94,2]{0,1:T(2,128)S(1)}, f32[94,2]{0,1:T(2,128)}, u32[]{:S(2)}) copy-start(f32[94,2]{0,1:T(2,128)} %get-tuple-element.524) | copy-start | bytes 2260 | tf_op jit(solution)/shard_map/while
  258.5 5.5 %copy-start.1 = (f32[94,2]{0,1:T(2,128)S(1)}, f32[94,2]{0,1:T(2,128)}, u32[]{:S(2)}) copy-start(f32[94,2]{0,1:T(2,128)} %get-tuple-element.524) | copy-start | bytes 2260 | tf_op jit(solution)/shard_map/while
  265.9 5.5 %copy-start.1 = (f32[94,2]{0,1:T(2,128)S(1)}, f32[94,2]{0,1:T(2,128)}, u32[]{:S(2)}) copy-start(f32[94,2]{0,1:T(2,128)} %get-tuple-element.524) | copy-start | bytes 2260 | tf_op jit(solution)/shard_map/while
  273.2 5.5 %copy-start.1 = (f32[94,2]{0,1:T(2,128)S(1)}, f32[94,2]{0,1:T(2,128)}, u32[]{:S(2)}) copy-start(f32[94,2]{0,1:T(2,128)} %get-tuple-element.524) | copy-start | bytes 2260 | tf_op jit(solution)/shard_map/while
  280.6 5.5 %copy-start.1 = (f32[94,2]{0,1:T(2,128)S(1)}, f32[94,2]{0,1:T(2,128)}, u32[]{:S(2)}) copy-start(f32[94,2]{0,1:T(2,128)} %get-tuple-element.524) | copy-start | bytes 2260 | tf_op jit(solution)/shard_map/while
  287.9 5.5 %copy-start.1 = (f32[94,2]{0,1:T(2,128)S(1)}, f32[94,2]{0,1:T(2,128)}, u32[]{:S(2)}) copy-start(f32[94,2]{0,1:T(2,128)} %get-tuple-element.524) | copy-start | bytes 2260 | tf_op jit(solution)/shard_map/while
  295.3 5.5 %copy-start.1 = (f32[94,2]{0,1:T(2,128)S(1)}, f32[94,2]{0,1:T(2,128)}, u32[]{:S(2)}) copy-start(f32[94,2]{0,1:T(2,128)} %get-tuple-element.524) | copy-start | bytes 2260 | tf_op jit(solution)/shard_map/while
  302.6 5.5 %copy-start.1 = (f32[94,2]{0,1:T(2,128)S(1)}, f32[94,2]{0,1:T(2,128)}, u32[]{:S(2)}) copy-start(f32[94,2]{0,1:T(2,128)} %get-tuple-element.524) | copy-start | bytes 2260 | tf_op jit(solution)/shard_map/while
  310.0 5.5 %copy-start.1 = (f32[94,2]{0,1:T(2,128)S(1)}, f32[94,2]{0,1:T(2,128)}, u32[]{:S(2)}) copy-start(f32[94,2]{0,1:T(2,128)} %get-tuple-element.524) | copy-start | bytes 2260 | tf_op jit(solution)/shard_map/while
  (2 other events, 6.4 us)
Sparse Core Ops, SparseCore 0:
  139.8 57.4 all-gather.1
where the time goes:
time: 329 us; the launch traced here: 328 us
  matrix products  87.8 us (27%)
  waiting for transfers between devices  61.6 us (19%)
  blocking collectives  55.7 us (17%)
  local copies, waits for them, and re-layouts  52.7 us (16%)
  other arithmetic  24.8 us (8%)
  starting transfers between devices  19 us (6%)
  between operations  14.3 us (4%)
  loops' own time  12.1 us (4%)
    conv_general_dilated x16, matrix products, block_value(): lax.conv_general_dilated(visiting, kernel, (LAG_STEP,), 'VALID', dimensio...  79 us
    unnamed x1, blocking collectives  55.7 us
    all_gather x1, waiting for transfers between devices, local(): lax.all_gather(centered, 'vert', axis=0, tiled=True)  54.5 us
    dynamic_slice x32, local copies, waits for them, and re-layouts, add_block(): visiting = lax.dynamic_slice_in_dim(piece, block_idx * par_dev, par_dev, 0)  17.8 us
    ppermute x2, starting transfers between devices, extended_2(): lax.ppermute(tail, axis, [(i, (i + 1) % count) for i in range(ends)])  12.9 us
    dynamic_update_slice x16, other arithmetic, add_block(): lax.dynamic_update_slice(total, guarded(visiting, first)[None], (slot, ze...  11.8 us
    another operation x1, loops' own time, local(): lax.map(one_block, jnp.arange(par_dev * lax.axis_size('vert') // par_dev,...  11 us
    dynamic_slice x16, local copies, waits for them, and re-layouts, local(): lax.map(one_block, jnp.arange(par_dev * lax.axis_size('vert') // par_dev,...  9.38 us
  transfers between devices with their start and end apart: 6, of which 3 were waited for; matrix products, arithmetic and copies ran while one was open for 2% of the time, Pallas kernels for 0%

commit v1 on v0

--- a/solution.py
+++ b/solution.py
@@ -153,7 +153,13 @@
     own_ext = extended_2(own_env, (("tm", 2),), LAG)
     centered, own_middle, own_spread = centered_rows(own_ext, t_dev)
     fold_rows = make_fold(own_middle, own_spread, owner_start, par_dev, t_dev)
-    blocks = fold_rows(empty, lax.all_gather(centered, "vert", axis=0, tiled=True), jnp.int32(0))
+    blocks = fold_rows(
+        empty,
+        jnp.concatenate(
+            lax.all_to_all(jnp.stack([centered] * lax.axis_size("vert")), "vert", 0, 0), axis=0
+        ),
+        jnp.int32(0),
+    )
     coupling = blocks.transpose(1, 2, 0, 3).reshape(BANDS, par_dev, total_par)
     return coupling[None]
 

time: 329 us -> 311 us (0.945); the launches traced: 328 us -> 306 us
  waiting for transfers between devices: 61.6 us -> 45.7 us
  between operations: 14.3 us -> 0.96 us
  starting transfers between devices: 19 us -> 26.4 us
    all_gather x1 -> x0, waiting for transfers between devices: 54.5 us -> none  [local(): lax.all_gather(centered, 'vert', axis=0, tiled=True)]
    all_to_all x0 -> x1, waiting for transfers between devices: none -> 38.4 us  [local(): lax.all_to_all(jnp.stack([centered] * lax.axis_size('vert')), 'vert', 0, 0)]
    all_to_all x0 -> x1, starting transfers between devices: none -> 5.1 us  [local(): lax.all_to_all(jnp.stack([centered] * lax.axis_size('vert')), 'vert', 0, 0)]
where the time goes in v1:
time: 311 us; the launch traced here: 306 us
  matrix products  87.8 us (28%)
  blocking collectives  55.7 us (18%)
  local copies, waits for them, and re-layouts  53.8 us (17%)
  waiting for transfers between devices  45.7 us (15%)
  starting transfers between devices  26.4 us (8%)
  other arithmetic  23.3 us (7%)
  loops' own time  12.1 us (4%)
    conv_general_dilated x16, matrix products, block_value(): lax.conv_general_dilated(visiting, kernel, (LAG_STEP,), 'VALID', dimensio...  79 us
    unnamed x1, blocking collectives  55.7 us
    all_to_all x1, waiting for transfers between devices, local(): lax.all_to_all(jnp.stack([centered] * lax.axis_size('vert')), 'vert', 0, 0)  38.4 us
    dynamic_slice x32, local copies, waits for them, and re-layouts, add_block(): visiting = lax.dynamic_slice_in_dim(piece, block_idx * par_dev, par_dev, 0)  17.8 us
    ppermute x2, starting transfers between devices, extended_2(): lax.ppermute(tail, axis, [(i, (i + 1) % count) for i in range(ends)])  15.6 us
    dynamic_update_slice x16, other arithmetic, add_block(): lax.dynamic_update_slice(total, guarded(visiting, first)[None], (slot, ze...  11.9 us
    another operation x1, loops' own time, local(): lax.map(one_block, jnp.arange(par_dev * lax.axis_size('vert') // par_dev,...  11 us
    dynamic_slice x16, local copies, waits for them, and re-layouts, local(): lax.map(one_block, jnp.arange(par_dev * lax.axis_size('vert') // par_dev,...  9.38 us
  transfers between devices with their start and end apart: 6, of which 3 were waited for; matrix products, arithmetic and copies ran while one was open for 2% of the time, Pallas kernels for 0%

profile of v1, /device:TPU:1, one launch (start us, length us, event | category | flops | bytes accessed | tf_op | source)
XLA Modules:
  0.0 305.7 jit_solution(13466340684246284900)
XLA Ops:
  2.0 4.9 %collective-permute-start = (bf16[1280,64]{1,0:T(8,128)(2,1)}, bf16[1280,64]{1,0:T(8,128)(2,1)}, u32[]{:S(2)}, u32[]{:S(2)}) collective-permute-start(bf16[1280,64]{1,0:T(8,128)(2,1)} %get-tuple-element.348), channel_id=1, source_target_pairs={{0,1},{1,2},{2,3},{3,4},{4,5},{5,6},{6,7},{7,8},{8,9},{9,10},{10,1... | collective-permute-start | bytes 491528 | tf_op jit(solution)/shard_map/ppermute | solution.py:28
  17.5 12.1 %while.38 = (s32[]{:T(128)}, bf16[10,128,2,128]{3,2,1,0:T(2,128)(2,1)}, bf16[10,128,256]{2,1,0:T(8,128)(2,1)S(1)}, bf16[256,768]{0,1:T(8,128)(2,1)S(1)}, bf16[2,192,128]{2,1,0:T(8,128)(2,1)S(1)}, /*index=5*/s32[]{:T(128)}) while((s32[]{:T(128)}, bf16[10,128,2,128]{3,2,1,0:T(2,128)(2,1)}, bf16[10,128,256]{2,1,0:T(8,128)(2,1)S(1)}, ...), condition=%wide.region_1.2_spmd, body=%wide.region_0.1_spmd.sunk | while | flops 63143936 | bytes 1540681 | solution.py:129
  30.7 27.9 %while.39 = (s32[]{:T(128)}, f32[16,94,256]{2,1,0:T(8,128)S(1)}, s32[3,1280]{1,0:T(4,128)S(1)}, s32[16]{0:T(128)S(1)}, bf16[1280,256]{1,0:T(8,128)(2,1)S(1)}, /*index=5*/s32[]{:T(128)}, s32[1]{0:T(128)}) while((s32[]{:T(128)}, f32[16,94,256]{2,1,0:T(8,128)S(1)}, s32[3,1280]{1,0:T(4,128)S(1)}, s32[16]{0:T(128)S(1)}, ...), condition=%wide.region_4.5_spmd, body=%wide.region_2.4_spmd.sunk | while | flops 62566496 | bytes 1256285 | solution.py:143
  58.8 55.7 %fusion.2 = f32[96,256]{1,0:T(8,128)S(1)} fusion(f32[1504,256]{1,0:T(8,128)S(1)} %reshape.157), kind=kCustom, calls=%all-reduce-scatter | all-reduce-scatter fusion | flops 393217 | bytes 1639424
  117.8 10.7 %collective-permute-start.2 = (f32[94,2,64]{2,1,0:T(2,128)S(1)}, f32[94,2,64]{2,1,0:T(2,128)S(1)}, u32[]{:S(2)}, u32[]{:S(2)}) collective-permute-start(f32[94,2,64]{2,1,0:T(2,128)S(1)} %get-tuple-element.350), channel_id=1, source_target_pairs={{0,1},{1,2},{2,3},{3,4},{4,5},{5,6},{6,7},{7,8},{8,9},{9,10},{10,1... | collective-permute-start | bytes 144392 | tf_op jit(solution)/shard_map/ppermute | solution.py:28
  136.8 5.1 %all-to-all-start = ((bf16[16,94,2,256]{3,2,1,0:T(2,128)(2,1)}), bf16[16,94,2,256]{3,2,1,0:T(2,128)(2,1)}, u32[]{:S(2)}, u32[]{:S(2)}) async-start(bf16[16,94,2,256]{3,2,1,0:T(2,128)(2,1)} %stack.2), calls=%async_computation | async-start | bytes 3080192 | tf_op jit(solution)/shard_map/all_to_all | solution.py:159
  143.2 38.4 %all-to-all-done = bf16[16,94,2,256]{3,2,1,0:T(2,128)(2,1)} async-done(((bf16[16,94,2,256]{3,2,1,0:T(2,128)(2,1)}), bf16[16,94,2,256]{3,2,1,0:T(2,128)(2,1)}, u32[]{:S(2)}, u32[]{:S(2)}) %all-to-all-start) | async-done | bytes 1540128 | tf_op jit(solution)/shard_map/all_to_all | solution.py:159
  183.0 117.7 %while.40 = (s32[]{:T(128)}, f32[16,2,94,94]{3,2,1,0:T(8,128)}, bf16[1504,2,256]{2,1,0:T(2,128)(2,1)}, bf16[188,1,128]{0,2,1:T(8,128)(2,1)S(1)}, f32[94,2]{0,1:T...) while((s32[]{:T(128)}, f32[16,2,94,94]{3,2,1,0:T(8,128)}, ...), condition=%wide.region_11.12_spmd.clone, body=%wide.region_8.11_spmd.clone.sunk | while | flops 1172045696 | bytes 1180199 | solution.py:99
  184.1 4.9 %multiply_reduce_fusion.5 = f32[94,188]{1,0:T(8,128)S(1)} fusion(bf16[94,2,256]{0,1,2:T(2,128)(2,1)S(1)} %copy.70, s32[188]{0:T(256)S(1)} %get-tuple-element.532, bf16[188,128]{0,1:T(8,128)(2,1)S(1)} %bitcast.105), kind=kOutput, calls=%fused_computation.18.clone.1 | convolution fusion | flops 1171838208 | bytes 215824 | tf_op jit(solution)/shard_map/while/body/eval_jaxpr/conv_general_dilated | solution.py:65
  191.5 4.9 %multiply_reduce_fusion.5 = f32[94,188]{1,0:T(8,128)S(1)} fusion(bf16[94,2,256]{0,1,2:T(2,128)(2,1)S(1)} %copy.70, s32[188]{0:T(256)S(1)} %get-tuple-element.532, bf16[188,128]{0,1:T(8,128)(2,1)S(1)} %bitcast.105), kind=kOutput, calls=%fused_computation.18.clone.1 | convolution fusion | flops 1171838208 | bytes 215824 | tf_op jit(solution)/shard_map/while/body/eval_jaxpr/conv_general_dilated | solution.py:65
  198.8 4.9 %multiply_reduce_fusion.5 = f32[94,188]{1,0:T(8,128)S(1)} fusion(bf16[94,2,256]{0,1,2:T(2,128)(2,1)S(1)} %copy.70, s32[188]{0:T(256)S(1)} %get-tuple-element.532, bf16[188,128]{0,1:T(8,128)(2,1)S(1)} %bitcast.105), kind=kOutput, calls=%fused_computation.18.clone.1 | convolution fusion | flops 1171838208 | bytes 215824 | tf_op jit(solution)/shard_map/while/body/eval_jaxpr/conv_general_dilated | solution.py:65
  206.2 4.9 %multiply_reduce_fusion.5 = f32[94,188]{1,0:T(8,128)S(1)} fusion(bf16[94,2,256]{0,1,2:T(2,128)(2,1)S(1)} %copy.70, s32[188]{0:T(256)S(1)} %get-tuple-element.532, bf16[188,128]{0,1:T(8,128)(2,1)S(1)} %bitcast.105), kind=kOutput, calls=%fused_computation.18.clone.1 | convolution fusion | flops 1171838208 | bytes 215824 | tf_op jit(solution)/shard_map/while/body/eval_jaxpr/conv_general_dilated | solution.py:65
  213.5 4.9 %multiply_reduce_fusion.5 = f32[94,188]{1,0:T(8,128)S(1)} fusion(bf16[94,2,256]{0,1,2:T(2,128)(2,1)S(1)} %copy.70, s32[188]{0:T(256)S(1)} %get-tuple-element.532, bf16[188,128]{0,1:T(8,128)(2,1)S(1)} %bitcast.105), kind=kOutput, calls=%fused_computation.18.clone.1 | convolution fusion | flops 1171838208 | bytes 215824 | tf_op jit(solution)/shard_map/while/body/eval_jaxpr/conv_general_dilated | solution.py:65
  220.9 4.9 %multiply_reduce_fusion.5 = f32[94,188]{1,0:T(8,128)S(1)} fusion(bf16[94,2,256]{0,1,2:T(2,128)(2,1)S(1)} %copy.70, s32[188]{0:T(256)S(1)} %get-tuple-element.532, bf16[188,128]{0,1:T(8,128)(2,1)S(1)} %bitcast.105), kind=kOutput, calls=%fused_computation.18.clone.1 | convolution fusion | flops 1171838208 | bytes 215824 | tf_op jit(solution)/shard_map/while/body/eval_jaxpr/conv_general_dilated | solution.py:65
  228.2 4.9 %multiply_reduce_fusion.5 = f32[94,188]{1,0:T(8,128)S(1)} fusion(bf16[94,2,256]{0,1,2:T(2,128)(2,1)S(1)} %copy.70, s32[188]{0:T(256)S(1)} %get-tuple-element.532, bf16[188,128]{0,1:T(8,128)(2,1)S(1)} %bitcast.105), kind=kOutput, calls=%fused_computation.18.clone.1 | convolution fusion | flops 1171838208 | bytes 215824 | tf_op jit(solution)/shard_map/while/body/eval_jaxpr/conv_general_dilated | solution.py:65
  235.6 4.9 %multiply_reduce_fusion.5 = f32[94,188]{1,0:T(8,128)S(1)} fusion(bf16[94,2,256]{0,1,2:T(2,128)(2,1)S(1)} %copy.70, s32[188]{0:T(256)S(1)} %get-tuple-element.532, bf16[188,128]{0,1:T(8,128)(2,1)S(1)} %bitcast.105), kind=kOutput, calls=%fused_computation.18.clone.1 | convolution fusion | flops 1171838208 | bytes 215824 | tf_op jit(solution)/shard_map/while/body/eval_jaxpr/conv_general_dilated | solution.py:65
  243.0 4.9 %multiply_reduce_fusion.5 = f32[94,188]{1,0:T(8,128)S(1)} fusion(bf16[94,2,256]{0,1,2:T(2,128)(2,1)S(1)} %copy.70, s32[188]{0:T(256)S(1)} %get-tuple-element.532, bf16[188,128]{0,1:T(8,128)(2,1)S(1)} %bitcast.105), kind=kOutput, calls=%fused_computation.18.clone.1 | convolution fusion | flops 1171838208 | bytes 215824 | tf_op jit(solution)/shard_map/while/body/eval_jaxpr/conv_general_dilated | solution.py:65
  250.3 4.9 %multiply_reduce_fusion.5 = f32[94,188]{1,0:T(8,128)S(1)} fusion(bf16[94,2,256]{0,1,2:T(2,128)(2,1)S(1)} %copy.70, s32[188]{0:T(256)S(1)} %get-tuple-element.532, bf16[188,128]{0,1:T(8,128)(2,1)S(1)} %bitcast.105), kind=kOutput, calls=%fused_computation.18.clone.1 | convolution fusion | flops 1171838208 | bytes 215824 | tf_op jit(solution)/shard_map/while/body/eval_jaxpr/conv_general_dilated | solution.py:65
  257.7 4.9 %multiply_reduce_fusion.5 = f32[94,188]{1,0:T(8,128)S(1)} fusion(bf16[94,2,256]{0,1,2:T(2,128)(2,1)S(1)} %copy.70, s32[188]{0:T(256)S(1)} %get-tuple-element.532, bf16[188,128]{0,1:T(8,128)(2,1)S(1)} %bitcast.105), kind=kOutput, calls=%fused_computation.18.clone.1 | convolution fusion | flops 1171838208 | bytes 215824 | tf_op jit(solution)/shard_map/while/body/eval_jaxpr/conv_general_dilated | solution.py:65
  265.0 4.9 %multiply_reduce_fusion.5 = f32[94,188]{1,0:T(8,128)S(1)} fusion(bf16[94,2,256]{0,1,2:T(2,128)(2,1)S(1)} %copy.70, s32[188]{0:T(256)S(1)} %get-tuple-element.532, bf16[188,128]{0,1:T(8,128)(2,1)S(1)} %bitcast.105), kind=kOutput, calls=%fused_computation.18.clone.1 | convolution fusion | flops 1171838208 | bytes 215824 | tf_op jit(solution)/shard_map/while/body/eval_jaxpr/conv_general_dilated | solution.py:65
  272.4 4.9 %multiply_reduce_fusion.5 = f32[94,188]{1,0:T(8,128)S(1)} fusion(bf16[94,2,256]{0,1,2:T(2,128)(2,1)S(1)} %copy.70, s32[188]{0:T(256)S(1)} %get-tuple-element.532, bf16[188,128]{0,1:T(8,128)(2,1)S(1)} %bitcast.105), kind=kOutput, calls=%fused_computation.18.clone.1 | convolution fusion | flops 1171838208 | bytes 215824 | tf_op jit(solution)/shard_map/while/body/eval_jaxpr/conv_general_dilated | solution.py:65
  279.7 4.9 %multiply_reduce_fusion.5 = f32[94,188]{1,0:T(8,128)S(1)} fusion(bf16[94,2,256]{0,1,2:T(2,128)(2,1)S(1)} %copy.70, s32[188]{0:T(256)S(1)} %get-tuple-element.532, bf16[188,128]{0,1:T(8,128)(2,1)S(1)} %bitcast.105), kind=kOutput, calls=%fused_computation.18.clone.1 | convolution fusion | flops 1171838208 | bytes 215824 | tf_op jit(solution)/shard_map/while/body/eval_jaxpr/conv_general_dilated | solution.py:65
  287.1 4.9 %multiply_reduce_fusion.5 = f32[94,188]{1,0:T(8,128)S(1)} fusion(bf16[94,2,256]{0,1,2:T(2,128)(2,1)S(1)} %copy.70, s32[188]{0:T(256)S(1)} %get-tuple-element.532, bf16[188,128]{0,1:T(8,128)(2,1)S(1)} %bitcast.105), kind=kOutput, calls=%fused_computation.18.clone.1 | convolution fusion | flops 1171838208 | bytes 215824 | tf_op jit(solution)/shard_map/while/body/eval_jaxpr/conv_general_dilated | solution.py:65
  294.4 4.9 %multiply_reduce_fusion.5 = f32[94,188]{1,0:T(8,128)S(1)} fusion(bf16[94,2,256]{0,1,2:T(2,128)(2,1)S(1)} %copy.70, s32[188]{0:T(256)S(1)} %get-tuple-element.532, bf16[188,128]{0,1:T(8,128)(2,1)S(1)} %bitcast.105), kind=kOutput, calls=%fused_computation.18.clone.1 | convolution fusion | flops 1171838208 | bytes 215824 | tf_op jit(solution)/shard_map/while/body/eval_jaxpr/conv_general_dilated | solution.py:65
  (340 shorter events, 98.8 us)
Async XLA Ops:
  2.0 10.6 %collective-permute-start = (bf16[1280,64]{1,0:T(8,128)(2,1)}, bf16[1280,64]{1,0:T(8,128)(2,1)}, u32[]{:S(2)}, u32[]{:S(2)}) collective-permute-start(bf16[1280,64]{1,0:T(8,128)(2,1)} %get-tuple-element.348), channel_id=1, source_target_pairs={{0,1},{1,2},{2,3},{3,4},{4,5},{5,6},{6,7},{7,8},{8,9},{9,10},{10,1... | collective-permute-start | bytes 491528 | tf_op jit(solution)/shard_map/ppermute | solution.py:28
  6.9 9.1 %collective-permute-start.1 = (bf16[1280,64]{1,0:T(8,128)(2,1)S(1)}, bf16[1280,64]{1,0:T(8,128)(2,1)}, u32[]{:S(2)}, u32[]{:S(2)}) collective-permute-start(bf16[1280,64]{1,0:T(8,128)(2,1)S(1)} %get-tuple-element.349), channel_id=1, source_target_pairs={{1,0},{2,1},{3,2},{4,3},{5,4},{6,5},{7,6},{8,7},{9,8},{10,9},{11,1... | collective-permute-start | bytes 491528 | tf_op jit(solution)/shard_map/ppermute | solution.py:30
  58.8 57.2 %copy-start.3 = (u32[256]{0:T(256)S(1)}, u32[256]{0:T(256)}, u32[]{:S(2)}) copy-start(u32[256]{0:T(256)} %constant.228) | copy-start | bytes 3076
  114.5 2.8 collective-permute-start.4
  117.8 12.8 %collective-permute-start.2 = (f32[94,2,64]{2,1,0:T(2,128)S(1)}, f32[94,2,64]{2,1,0:T(2,128)S(1)}, u32[]{:S(2)}, u32[]{:S(2)}) collective-permute-start(f32[94,2,64]{2,1,0:T(2,128)S(1)} %get-tuple-element.350), channel_id=1, source_target_pairs={{0,1},{1,2},{2,3},{3,4},{4,5},{5,6},{6,7},{7,8},{8,9},{9,10},{10,1... | collective-permute-start | bytes 144392 | tf_op jit(solution)/shard_map/ppermute | solution.py:28
  128.5 5.9 %collective-permute-start.3 = (f32[94,2,64]{2,1,0:T(2,128)S(1)}, f32[94,2,64]{2,1,0:T(2,128)S(1)}, u32[]{:S(2)}, u32[]{:S(2)}) collective-permute-start(f32[94,2,64]{2,1,0:T(2,128)S(1)} %get-tuple-element.351), channel_id=1, source_target_pairs={{1,0},{2,1},{3,2},{4,3},{5,4},{6,5},{7,6},{8,7},{9,8},{10,9},{11,1... | collective-permute-start | bytes 144392 | tf_op jit(solution)/shard_map/ppermute | solution.py:30
  136.8 44.8 %all-to-all-start = ((bf16[16,94,2,256]{3,2,1,0:T(2,128)(2,1)}), bf16[16,94,2,256]{3,2,1,0:T(2,128)(2,1)}, u32[]{:S(2)}, u32[]{:S(2)}) async-start(bf16[16,94,2,256]{3,2,1,0:T(2,128)(2,1)} %stack.2), calls=%async_computation | async-start | bytes 3080192 | tf_op jit(solution)/shard_map/all_to_all | solution.py:159
  141.9 41.1 %copy-start.4 = (s32[188]{0:T(256)S(1)}, s32[188]{0:T(256)}, u32[]{:S(2)}) copy-start(s32[188]{0:T(256)} %constant.197.clone.2) | copy-start | bytes 2260
  184.1 5.5 %copy-start.1 = (f32[94,2]{0,1:T(2,128)S(1)}, f32[94,2]{0,1:T(2,128)}, u32[]{:S(2)}) copy-start(f32[94,2]{0,1:T(2,128)} %get-tuple-element.524) | copy-start | bytes 2260 | tf_op jit(solution)/shard_map/while
  191.5 5.5 %copy-start.1 = (f32[94,2]{0,1:T(2,128)S(1)}, f32[94,2]{0,1:T(2,128)}, u32[]{:S(2)}) copy-start(f32[94,2]{0,1:T(2,128)} %get-tuple-element.524) | copy-start | bytes 2260 | tf_op jit(solution)/shard_map/while
  198.8 5.5 %copy-start.1 = (f32[94,2]{0,1:T(2,128)S(1)}, f32[94,2]{0,1:T(2,128)}, u32[]{:S(2)}) copy-start(f32[94,2]{0,1:T(2,128)} %get-tuple-element.524) | copy-start | bytes 2260 | tf_op jit(solution)/shard_map/while
  206.2 5.5 %copy-start.1 = (f32[94,2]{0,1:T(2,128)S(1)}, f32[94,2]{0,1:T(2,128)}, u32[]{:S(2)}) copy-start(f32[94,2]{0,1:T(2,128)} %get-tuple-element.524) | copy-start | bytes 2260 | tf_op jit(solution)/shard_map/while
  213.5 5.5 %copy-start.1 = (f32[94,2]{0,1:T(2,128)S(1)}, f32[94,2]{0,1:T(2,128)}, u32[]{:S(2)}) copy-start(f32[94,2]{0,1:T(2,128)} %get-tuple-element.524) | copy-start | bytes 2260 | tf_op jit(solution)/shard_map/while
  220.9 5.5 %copy-start.1 = (f32[94,2]{0,1:T(2,128)S(1)}, f32[94,2]{0,1:T(2,128)}, u32[]{:S(2)}) copy-start(f32[94,2]{0,1:T(2,128)} %get-tuple-element.524) | copy-start | bytes 2260 | tf_op jit(solution)/shard_map/while
  228.2 5.5 %copy-start.1 = (f32[94,2]{0,1:T(2,128)S(1)}, f32[94,2]{0,1:T(2,128)}, u32[]{:S(2)}) copy-start(f32[94,2]{0,1:T(2,128)} %get-tuple-element.524) | copy-start | bytes 2260 | tf_op jit(solution)/shard_map/while
  235.6 5.5 %copy-start.1 = (f32[94,2]{0,1:T(2,128)S(1)}, f32[94,2]{0,1:T(2,128)}, u32[]{:S(2)}) copy-start(f32[94,2]{0,1:T(2,128)} %get-tuple-element.524) | copy-start | bytes 2260 | tf_op jit(solution)/shard_map/while
  242.9 5.5 %copy-start.1 = (f32[94,2]{0,1:T(2,128)S(1)}, f32[94,2]{0,1:T(2,128)}, u32[]{:S(2)}) copy-start(f32[94,2]{0,1:T(2,128)} %get-tuple-element.524) | copy-start | bytes 2260 | tf_op jit(solution)/shard_map/while
  250.3 5.5 %copy-start.1 = (f32[94,2]{0,1:T(2,128)S(1)}, f32[94,2]{0,1:T(2,128)}, u32[]{:S(2)}) copy-start(f32[94,2]{0,1:T(2,128)} %get-tuple-element.524) | copy-start | bytes 2260 | tf_op jit(solution)/shard_map/while
  257.6 5.5 %copy-start.1 = (f32[94,2]{0,1:T(2,128)S(1)}, f32[94,2]{0,1:T(2,128)}, u32[]{:S(2)}) copy-start(f32[94,2]{0,1:T(2,128)} %get-tuple-element.524) | copy-start | bytes 2260 | tf_op jit(solution)/shard_map/while
  265.0 5.5 %copy-start.1 = (f32[94,2]{0,1:T(2,128)S(1)}, f32[94,2]{0,1:T(2,128)}, u32[]{:S(2)}) copy-start(f32[94,2]{0,1:T(2,128)} %get-tuple-element.524) | copy-start | bytes 2260 | tf_op jit(solution)/shard_map/while
  272.3 5.5 %copy-start.1 = (f32[94,2]{0,1:T(2,128)S(1)}, f32[94,2]{0,1:T(2,128)}, u32[]{:S(2)}) copy-start(f32[94,2]{0,1:T(2,128)} %get-tuple-element.524) | copy-start | bytes 2260 | tf_op jit(solution)/shard_map/while
  279.7 5.5 %copy-start.1 = (f32[94,2]{0,1:T(2,128)S(1)}, f32[94,2]{0,1:T(2,128)}, u32[]{:S(2)}) copy-start(f32[94,2]{0,1:T(2,128)} %get-tuple-element.524) | copy-start | bytes 2260 | tf_op jit(solution)/shard_map/while
  287.1 5.5 %copy-start.1 = (f32[94,2]{0,1:T(2,128)S(1)}, f32[94,2]{0,1:T(2,128)}, u32[]{:S(2)}) copy-start(f32[94,2]{0,1:T(2,128)} %get-tuple-element.524) | copy-start | bytes 2260 | tf_op jit(solution)/shard_map/while
  294.4 5.5 %copy-start.1 = (f32[94,2]{0,1:T(2,128)S(1)}, f32[94,2]{0,1:T(2,128)}, u32[]{:S(2)}) copy-start(f32[94,2]{0,1:T(2,128)} %get-tuple-element.524) | copy-start | bytes 2260 | tf_op jit(solution)/shard_map/while
  (2 other events, 6.4 us)
